TPU v7x, 32 devices: a whole 2x2x4 slice. The times are simulated.
32 devices in a mesh: groups: 2 (over y), dp: 16 (over z, x, core).
Axes of the slice: x: 2, y: 2, z: 4, core: 2. Of those that a mesh axis runs over, the one named last changes fastest.
Arguments:
- queries: bfloat16 [16384, 4096], P(('groups', 'dp')), parts along dimension 0, may hold values from -100 to 100
- resp_kv: bfloat16 [16384, 2, 512], P(('groups', 'dp')), parts along dimension 0, may hold values from -6 to 6
- prompt_kv: bfloat16 [8192, 2, 512], P(('groups', 'dp')), parts along dimension 0, may hold values from -6 to 6
- groups: int32 [64], P(('groups', 'dp')), parts along dimension 0, may hold values from 0 to 15, as said below
- resp_lengths: int32 [64], P(('groups', 'dp')), parts along dimension 0, may hold values from 64 to 256, as said below
- prompt_lengths: int32 [32], P('groups'), parts along dimension 0, may hold values from 64 to 256, as said below
Outputs:
- attended: bfloat16 [16384, 4096], P(('groups', 'dp')), parts along dimension 0
There are 2 independent parts, one for each index of `groups`. A program takes and returns all parts, laid end to end along the dimension named above; each array names one. Nothing has to cross between parts.
Inputs may be any that keep to these rules, and one draw needn't show every extreme that they name: `groups`: entry n is the prompt whose rows response n reads; some prompts are read by many responses. `resp_lengths`: rows at and after the length are padding. `prompt_lengths`: key rows at and after the length are padding.
All inputs are finite; a program needn't handle non-finite values.
Results may differ from a plain program's by a relative error of at most 0.0043.
Values may be sent and summed in bfloat16 or wider, within the bound.
No kernel may reach another device: no remote copies, remote signals or barrier semaphores. Data moves between devices by JAX's collectives and lax.ppermute only.
A program may use at most 128 MiB of HBM per device.

v0:
```python
import functools
import math

import jax
import jax.numpy as jnp
from jax import lax
from jax.experimental import pallas as pl
from jax.experimental.pallas import tpu as pltpu
from jax.sharding import PartitionSpec as P

KV_HEADS = 4
HEAD_DIM = 128
TILE = 16
CHUNKS = 1

masked_score = -1e30
FOLD = math.log2(math.e) / math.sqrt(HEAD_DIM)


def pack_kernel(heads, devices, groups_ref, kv_ref, out_ref):
    slots = groups_ref.shape[0]
    tiles = 0
    for part in range(2):
        rows = kv_ref[:, part, :]
        for head in range(heads):
            block = rows[:, head * HEAD_DIM : (head + 1) * HEAD_DIM]
            out_ref[:, tiles * TILE : (tiles + 1) * TILE, :] = block.reshape(devices, TILE, HEAD_DIM)
            tiles += 1
    extra = out_ref.shape[1] - tiles * TILE
    if extra:
        lane = lax.broadcasted_iota(jnp.int32, (devices, extra, HEAD_DIM), 2)
        wanted = jnp.zeros((devices, extra, HEAD_DIM), jnp.float32)
        for slot in range(slots):
            wanted = jnp.where(lane == slot, groups_ref[slot].astype(jnp.float32), wanted)
        out_ref[:, tiles * TILE :, :] = wanted.astype(jnp.bfloat16)


def select_kernel(slots, rows, in_ref, out_ref, vec_ref, idx_ref, sem):
    devices = in_ref.shape[0]
    wanted = in_ref[:, rows:, :].astype(jnp.float32)
    vec_ref[...] = wanted[:, 0, :].astype(jnp.int32)
    copy = pltpu.make_async_copy(vec_ref, idx_ref, sem)
    copy.start()
    copy.wait()
    for target in range(devices):
        for slot in range(slots):
            out_ref[target, slot] = in_ref[idx_ref[target, slot], :rows, :]


def with_ones(values):
    return jnp.concatenate([values, jnp.ones(values.shape, values.dtype)], axis=1)


def own_kernel(per_group, q_ref, kv_ref, out_ref, lse_ref):
    size = q_ref.shape[0]
    half = size // 2
    keys = kv_ref[:, 0, :]
    values = with_ones(kv_ref[:, 1, :])
    row = lax.broadcasted_iota(jnp.int32, (half, half), 0)
    col = lax.broadcasted_iota(jnp.int32, (half, half), 1)
    causal = col <= row
    lane = lax.broadcasted_iota(jnp.int32, (half, HEAD_DIM), 1)
    for part in range(2):
        rows = slice(part * half, (part + 1) * half)
        seen = (part + 1) * half
        logs = jnp.zeros((half, HEAD_DIM), jnp.float32)
        for head in range(per_group):
            cols = slice(head * HEAD_DIM, (head + 1) * HEAD_DIM)
            score = lax.dot_general(
                q_ref[rows, cols],
                keys[:seen],
                (((1,), (1,)), ((), ())),
                preferred_element_type=jnp.float32,
            )
            last = jnp.where(causal, score[:, seen - half :], masked_score)
            score = last if part == 0 else jnp.concatenate([score[:, :half], last], axis=1)
            highest = jnp.max(score, axis=1, keepdims=True) * FOLD
            weight = jnp.exp2(score * FOLD - highest).astype(jnp.bfloat16)
            sums = jnp.dot(weight, values[:seen], preferred_element_type=jnp.float32)
            totals = sums[:, HEAD_DIM:]
            out_ref[rows, cols] = (sums[:, :HEAD_DIM] / totals).astype(out_ref.dtype)
            logs = jnp.where(lane == head, highest + jnp.log2(totals), logs)
        lse_ref[rows, :] = logs


def prompt_kernel(per_group, first, *refs):
    groups_ref, lives_ref, plens_ref, q_ref, own_ref, lse_ref, k_ref, v_ref = refs[:8]
    out_ref = refs[-1]
    size = q_ref.shape[0]
    half = size // 2
    slot = pl.program_id(0)
    keys = k_ref[...].reshape(-1, HEAD_DIM)
    values = with_ones(v_ref[...].reshape(-1, HEAD_DIM))
    live = plens_ref[groups_ref[slot]]
    rows_live = lives_ref[slot]
    plen = keys.shape[0]
    mask = lax.broadcasted_iota(jnp.int32, (half, plen), 1) < live
    for part in range(2):
        rows = slice(part * half, (part + 1) * half)
        row = lax.broadcasted_iota(jnp.int32, (half, HEAD_DIM), 0) + part * half
        kept = row < rows_live
        for head in range(per_group):
            cols = slice(head * HEAD_DIM, (head + 1) * HEAD_DIM)
            score = lax.dot_general(
                q_ref[rows, cols],
                keys,
                (((1,), (1,)), ((), ())),
                preferred_element_type=jnp.float32,
            )
            score = jnp.where(mask, score, masked_score)
            own_log = lse_ref[rows, head : head + 1]
            highest = jnp.maximum(jnp.max(score, axis=1, keepdims=True) * FOLD, own_log)
            weight = jnp.exp2(score * FOLD - highest).astype(jnp.bfloat16)
            sums = jnp.dot(weight, values, preferred_element_type=jnp.float32)
            scale = jnp.exp2(own_log - highest)
            total = sums[:, HEAD_DIM:] + scale
            result = (sums[:, :HEAD_DIM] + scale * own_ref[rows, cols].astype(jnp.float32)) / total
            out_ref[rows, cols] = jnp.where(kept, result, 0.0).astype(out_ref.dtype)


def params(mib=40):
    return pltpu.CompilerParams(vmem_limit_bytes=mib * 1024 * 1024)


def fetch_fast(prompt_kv, groups, devices):
    slots = groups.shape[0]
    prompt_len = prompt_kv.shape[0]
    heads = KV_HEADS
    rows = 2 * heads * TILE
    extra = 8
    smem = pl.BlockSpec(memory_space=pltpu.SMEM)
    vmem = pl.BlockSpec(memory_space=pltpu.VMEM)
    packed = pl.pallas_call(
        functools.partial(pack_kernel, heads, devices),
        out_shape=jax.ShapeDtypeStruct((devices, rows + extra, HEAD_DIM), jnp.bfloat16),
        in_specs=[smem, vmem],
        out_specs=vmem,
        name="pack",
    )(groups, prompt_kv)
    spread = lax.all_to_all(packed, "dp", split_axis=0, concat_axis=0, tiled=True)
    chosen = pl.pallas_call(
        functools.partial(select_kernel, slots, rows),
        out_shape=jax.ShapeDtypeStruct((devices, slots, rows, HEAD_DIM), jnp.bfloat16),
        in_specs=[vmem],
        out_specs=vmem,
        scratch_shapes=[
            pltpu.VMEM((devices, HEAD_DIM), jnp.int32),
            pltpu.SMEM((devices, HEAD_DIM), jnp.int32),
            pltpu.SemaphoreType.DMA,
        ],
        name="select",
    )(spread)
    return lax.all_to_all(chosen, "dp", split_axis=0, concat_axis=0, tiled=True)


def fetch_plain(prompt_kv, groups, devices):
    slots = groups.shape[0]
    prompt_len, _, width = prompt_kv.shape
    sliver = prompt_len // devices
    wanted = lax.all_gather(groups, "dp", axis=0, tiled=True)
    by_prompt = lax.all_to_all(
        prompt_kv.reshape(devices, sliver, 2, width), "dp", split_axis=0, concat_axis=0, tiled=True
    )
    chosen = jnp.take(by_prompt, wanted, axis=0).reshape(devices, slots, sliver, 2, width)
    fetched = lax.all_to_all(chosen, "dp", split_axis=0, concat_axis=0, tiled=True)
    whole = jnp.transpose(fetched, (1, 0, 2, 3, 4)).reshape(slots, -1, TILE, 2, KV_HEADS, HEAD_DIM)
    whole = jnp.transpose(whole, (1, 0, 3, 4, 2, 5))
    return whole.reshape(whole.shape[0], slots, 2 * KV_HEADS * TILE, HEAD_DIM)


def on_device(queries, resp_kv, prompt_kv, groups, resp_lengths, prompt_lengths):
    devices = lax.axis_size("dp")
    slots = groups.shape[0]
    resp_len = queries.shape[0] // slots
    width = queries.shape[1] // KV_HEADS
    per_group = width // HEAD_DIM
    prompt_len = prompt_kv.shape[0]
    if prompt_len == devices * TILE:
        fetched = fetch_fast(prompt_kv, groups, devices)
    else:
        fetched = fetch_plain(prompt_kv, groups, devices)
    blocks = fetched.shape[0]

    q_spec = pl.BlockSpec((resp_len, width), lambda s, c, *_: (s, c))
    log_spec = pl.BlockSpec((resp_len, HEAD_DIM), lambda s, c, *_: (s, c))
    scores = queries.shape[0] * queries.shape[1] // HEAD_DIM * resp_len
    own, logs = pl.pallas_call(
        functools.partial(own_kernel, per_group),
        grid=(slots, KV_HEADS),
        out_shape=(
            jax.ShapeDtypeStruct(queries.shape, jnp.bfloat16),
            jax.ShapeDtypeStruct((queries.shape[0], KV_HEADS * HEAD_DIM), jnp.float32),
        ),
        in_specs=[q_spec, pl.BlockSpec((resp_len, 2, HEAD_DIM), lambda s, c: (s, 0, c))],
        out_specs=(q_spec, log_spec),
        compiler_params=params(),
        cost_estimate=pl.CostEstimate(
            flops=scores * HEAD_DIM * 4, bytes_accessed=queries.size * 4, transcendentals=scores
        ),
        name="own",
    )(queries, resp_kv)

    def tile_spec(offset):
        return pl.BlockSpec(
            (blocks, None, TILE, HEAD_DIM), lambda s, c, *_: (0, s, c + offset, 0)
        )

    return pl.pallas_call(
        functools.partial(prompt_kernel, per_group, 0),
        grid_spec=pltpu.PrefetchScalarGridSpec(
            num_scalar_prefetch=3,
            grid=(slots, KV_HEADS),
            in_specs=[q_spec, q_spec, log_spec, tile_spec(0), tile_spec(KV_HEADS)],
            out_specs=q_spec,
        ),
        out_shape=jax.ShapeDtypeStruct(queries.shape, jnp.bfloat16),
        compiler_params=params(),
        cost_estimate=pl.CostEstimate(
            flops=scores * HEAD_DIM * 4, bytes_accessed=queries.size * 6, transcendentals=scores
        ),
        name="prompt",
    )(groups, resp_lengths, prompt_lengths, queries, own, logs, fetched, fetched)


def solution(mesh):
    return jax.shard_map(
        on_device,
        mesh=mesh,
        in_specs=(
            P(("groups", "dp"), None),
            P(("groups", "dp"), None, None),
            P(("groups", "dp"), None, None),
            P(("groups", "dp")),
            P(("groups", "dp")),
            P("groups"),
        ),
        out_specs=P(("groups", "dp"), None),
        check_vma=False,
    )
```

profile of v0, /device:TPU:9, one launch (start us, length us, event | category | flops | bytes accessed | tf_op | source)
XLA Modules:
  0.0 87.1 jit_solution(13155939284336721677)
XLA Ops:
  0.0 0.0 copy-start.7
  0.0 3.8 %pack.1 = bf16[16,136,128]{2,1,0:T(8,128)(2,1)} custom-call(s32[2]{0:T(128)} %refs_0_.1, bf16[256,2,512]{2,1,0:T(2,128)(2,1)} %kv_ref.3), custom_call_target="tpu_custom_call" | custom-call | tf_op jit(solution)/shard_map/pack/pallas_call | solution.py:133
  3.8 22.0 %all_to_all.10.in_ref = bf16[16,136,128]{2,1,0:T(8,128)(2,1)} all-to-all(bf16[16,136,128]{2,1,0:T(8,128)(2,1)} %pack.1), channel_id=1, replica_groups=mesh['groups'=2,'dp'=16] {'dp'}, dimensions={0} | all-to-all | bytes 1114112 | tf_op jit(solution)/shard_map/all_to_all | solution.py:140
  25.8 2.8 %select.1 = bf16[16,2,128,128]{3,2,1,0:T(8,128)(2,1)} custom-call(bf16[16,136,128]{2,1,0:T(8,128)(2,1)} %all_to_all.10.in_ref), custom_call_target="tpu_custom_call" | custom-call | tf_op jit(solution)/shard_map/select/pallas_call | solution.py:141
  28.6 4.9 %all-to-all-start.1 = ((bf16[16,2,128,128]{3,2,1,0:T(8,128)(2,1)}), bf16[16,2,128,128]{3,2,1,0:T(8,128)(2,1)S(1)}, u32[]{:S(2)}, u32[]{:S(2)}) async-start(bf16[16,2,128,128]{3,2,1,0:T(8,128)(2,1)} %select.1), calls=%async_computation.1 | async-start | bytes 2097152 | tf_op jit(solution)/shard_map/all_to_all | solution.py:153
  33.5 0.0 copy-done.7
  33.5 0.0 copy-start
  33.5 2.2 %copy-done = bf16[512,4096]{1,0:T(8,128)(2,1)S(1)} copy-done((bf16[512,4096]{1,0:T(8,128)(2,1)S(1)}, bf16[512,4096]{1,0:T(8,128)(2,1)}, u32[]{:S(2)}) %copy-start) | copy-done | bytes 4194328
  35.7 0.0 copy-start.4
  35.7 0.0 copy-start.5
  35.7 0.0 copy-start.6
  35.7 22.5 %own.1 = (bf16[512,4096]{1,0:T(8,128)(2,1)S(1)}, f32[512,512]{1,0:T(8,128)S(1)}) custom-call(bf16[512,4096]{1,0:T(8,128)(2,1)S(1)} %copy-done, bf16[512,2,512]{2,1,0:T(2,128)(2,1)S(1)} %copy-done.7), custom_call_target="tpu_custom_call" | custom-call | flops 2147483648 | bytes 8388608 | tf_op jit(solution)/shard_map/own/pallas_call | solution.py:187
  58.2 0.0 copy-start.2
  58.2 2.0 %copy-done.2 = bf16[512,4096]{1,0:T(8,128)(2,1)} copy-done((bf16[512,4096]{1,0:T(8,128)(2,1)}, bf16[512,4096]{1,0:T(8,128)(2,1)S(1)}, u32[]{:S(2)}) %copy-start.2) | copy-done | bytes 4194328
  60.2 0.0 all-to-all-done.1.refs_6_.refs_7_
  60.2 0.0 copy-done.4
  60.2 0.0 copy-done.5
  60.2 0.0 copy-done.6
  60.2 0.0 copy-start.1
  60.2 2.2 %copy-done.1 = bf16[512,4096]{1,0:T(8,128)(2,1)S(1)} copy-done((bf16[512,4096]{1,0:T(8,128)(2,1)S(1)}, bf16[512,4096]{1,0:T(8,128)(2,1)}, u32[]{:S(2)}) %copy-start.1) | copy-done | bytes 4194328
  62.4 0.0 copy-start.3
  62.4 2.2 %copy-done.3 = bf16[512,4096]{1,0:T(8,128)(2,1)S(1)} copy-done((bf16[512,4096]{1,0:T(8,128)(2,1)S(1)}, bf16[512,4096]{1,0:T(8,128)(2,1)}, u32[]{:S(2)}) %copy-start.3) | copy-done | bytes 4194328
  64.6 22.5 %prompt.1 = bf16[512,4096]{1,0:T(8,128)(2,1)} custom-call(s32[2]{0:T(128)S(1)} %copy-done.4, s32[2]{0:T(128)S(1)} %copy-done.5, s32[16]{0:T(128)S(1)} %copy-done.6, bf16[512,4096]{1,0:T(8,128)(2,1)S(1)} %copy-done.1, bf16[512,4096]{1,0:T(8,128)(2,1)S(1)} %copy-done.3, f32[512,512]{1,0:T(8,128)S(1)} %get-tuple-element.8.refs_5_, ...), custom_call_target="tpu_custom_call" | custom-call | flops 2147483648 | bytes 12582912 | tf_op jit(solution)/shard_map/prompt/pallas_call | solution.py:208
Async XLA Ops:
  0.0 33.5 %copy-start.7 = (bf16[512,2,512]{2,1,0:T(2,128)(2,1)S(1)}, bf16[512,2,512]{2,1,0:T(2,128)(2,1)}, u32[]{:S(2)}) copy-start(bf16[512,2,512]{2,1,0:T(2,128)(2,1)} %kv_ref.2) | copy-start | bytes 3145732
  28.6 31.6 %all-to-all-start.1 = ((bf16[16,2,128,128]{3,2,1,0:T(8,128)(2,1)}), bf16[16,2,128,128]{3,2,1,0:T(8,128)(2,1)S(1)}, u32[]{:S(2)}, u32[]{:S(2)}) async-start(bf16[16,2,128,128]{3,2,1,0:T(8,128)(2,1)} %select.1), calls=%async_computation.1 | async-start | bytes 2097152 | tf_op jit(solution)/shard_map/all_to_all | solution.py:153
  33.5 2.2 %copy-start = (bf16[512,4096]{1,0:T(8,128)(2,1)S(1)}, bf16[512,4096]{1,0:T(8,128)(2,1)}, u32[]{:S(2)}) copy-start(bf16[512,4096]{1,0:T(8,128)(2,1)} %refs_3_.1) | copy-start | bytes 12582916
  35.7 24.5 %copy-start.4 = (s32[2]{0:T(128)S(1)}, s32[2]{0:T(128)}, u32[]{:S(2)}) copy-start(s32[2]{0:T(128)} %refs_0_.1) | copy-start | bytes 28
  35.7 24.5 %copy-start.5 = (s32[2]{0:T(128)S(1)}, s32[2]{0:T(128)}, u32[]{:S(2)}) copy-start(s32[2]{0:T(128)} %refs_1_.1) | copy-start | bytes 28
  35.7 24.5 %copy-start.6 = (s32[16]{0:T(128)S(1)}, s32[16]{0:T(128)}, u32[]{:S(2)}) copy-start(s32[16]{0:T(128)} %refs_2_.1) | copy-start | bytes 196
  58.2 2.0 %copy-start.2 = (bf16[512,4096]{1,0:T(8,128)(2,1)}, bf16[512,4096]{1,0:T(8,128)(2,1)S(1)}, u32[]{:S(2)}) copy-start(bf16[512,4096]{1,0:T(8,128)(2,1)S(1)} %get-tuple-element.7.refs_4_) | copy-start | bytes 12582916
  60.2 2.2 %copy-start.1 = (bf16[512,4096]{1,0:T(8,128)(2,1)S(1)}, bf16[512,4096]{1,0:T(8,128)(2,1)}, u32[]{:S(2)}) copy-start(bf16[512,4096]{1,0:T(8,128)(2,1)} %refs_3_.1) | copy-start | bytes 12582916
  62.4 2.2 %copy-start.3 = (bf16[512,4096]{1,0:T(8,128)(2,1)S(1)}, bf16[512,4096]{1,0:T(8,128)(2,1)}, u32[]{:S(2)}) copy-start(bf16[512,4096]{1,0:T(8,128)(2,1)} %copy-done.2) | copy-start | bytes 12582916
where the time goes:
time: 88.5 us; the launch traced here: 87.1 us
  Pallas kernels  51.5 us (58%)
  blocking collectives  22 us (25%)
  local copies, waits for them, and re-layouts  8.58 us (10%)
  starting transfers between devices  4.9 us (6%)
    pallas_call x1, Pallas kernels, on_device(): pl.pallas_call(functools.partial(prompt_kernel, per_group, 0), grid_spec=...  22.5 us
    pallas_call x1, Pallas kernels, on_device(): pl.pallas_call(functools.partial(own_kernel, per_group), grid=(slots, KV_...  22.5 us
    all_to_all x1, blocking collectives, fetch_fast(): lax.all_to_all(packed, 'dp', split_axis=0, concat_axis=0, tiled=True)  22 us
    unnamed x16, local copies, waits for them, and re-layouts  8.58 us
    all_to_all x1, starting transfers between devices, fetch_fast(): return lax.all_to_all(chosen, 'dp', split_axis=0, concat_axis=0, tiled=True)  4.9 us
    pallas_call x1, Pallas kernels, fetch_fast(): pl.pallas_call(functools.partial(pack_kernel, heads, devices), out_shape=...  3.77 us
    pallas_call x1, Pallas kernels, fetch_fast(): pl.pallas_call(functools.partial(select_kernel, slots, rows), out_shape=j...  2.79 us
  transfers between devices with their start and end apart: 1, of which 0 were waited for; matrix products, arithmetic and copies ran while one was open for 0% of the time, Pallas kernels for 26%

commit v1 on v0

v1 whole, which is shorter than its diff:
```python
import functools
import math

import jax
import jax.numpy as jnp
from jax import lax
from jax.experimental import pallas as pl
from jax.experimental.pallas import tpu as pltpu
from jax.sharding import PartitionSpec as P

KV_HEADS = 4
HEAD_DIM = 128
TILE = 16

masked_score = -1e30
FOLD = math.log2(math.e) / math.sqrt(HEAD_DIM)


def split_pairs(pairs):
    count = pairs.shape[0]
    half = count // 2
    row = lax.broadcasted_iota(jnp.int32, (count, count), 0)
    col = lax.broadcasted_iota(jnp.int32, (count, count), 1)
    source = jnp.where(row < half, 2 * row, 2 * (row - half) + 1)
    chosen = jnp.where(col == source, 1.0, 0.0).astype(pairs.dtype)
    return jnp.dot(chosen, pairs, preferred_element_type=jnp.float32).astype(pairs.dtype)


def pack_kernel(heads, devices, groups_ref, kv_ref, out_ref):
    slots = groups_ref.shape[0]
    count = kv_ref.shape[0]
    head = pl.program_id(0)
    split = split_pairs(kv_ref[...].reshape(2 * count, HEAD_DIM))
    for part in range(2):
        first = pl.multiple_of((part * heads + head) * TILE, TILE)
        out_ref[:, pl.ds(first, TILE), :] = split[part * count : (part + 1) * count].reshape(
            devices, TILE, HEAD_DIM
        )
    rows = 2 * heads * TILE
    extra = out_ref.shape[1] - rows
    if extra:

        @pl.when(head == 0)
        def _():
            lane = lax.broadcasted_iota(jnp.int32, (devices, extra, HEAD_DIM), 2)
            wanted = jnp.zeros((devices, extra, HEAD_DIM), jnp.float32)
            for slot in range(slots):
                wanted = jnp.where(lane == slot, groups_ref[slot].astype(jnp.float32), wanted)
            out_ref[:, rows:, :] = wanted.astype(jnp.bfloat16)


def select_kernel(slots, rows, in_ref, after_ref, out_ref, vec_ref, idx_ref, sem, sems):
    wanted = in_ref[:, rows:, :].astype(jnp.float32)
    vec_ref[...] = wanted[:, 0, :].astype(jnp.int32)
    copy = pltpu.make_async_copy(vec_ref, idx_ref, sem)
    copy.start()
    copy.wait()
    copies = []
    for target in range(in_ref.shape[0]):
        for slot in range(slots):
            copies.append(
                pltpu.make_async_copy(
                    in_ref.at[idx_ref[target, slot], pl.ds(0, rows)],
                    out_ref.at[target, slot],
                    sems.at[target, slot],
                )
            )
            copies[-1].start()
    for copy in copies:
        copy.wait()


def scores_of(keys, queries):
    return lax.dot_general(
        keys, queries, (((1,), (1,)), ((), ())), preferred_element_type=jnp.float32
    )


def with_ones(values):
    turned = jnp.transpose(values)
    return jnp.concatenate([turned, jnp.ones((TILE, turned.shape[1]), turned.dtype)], axis=0)


def own_kernel(per_group, q_ref, kv_ref, *refs):
    out_ref, top_ref, sum_ref = refs[-3:]
    size = q_ref.shape[0]
    half = size // 2
    split = split_pairs(kv_ref[...].reshape(2 * size, HEAD_DIM))
    keys = split[:size]
    values = with_ones(split[size:])
    key = lax.broadcasted_iota(jnp.int32, (half, half), 0)
    row = lax.broadcasted_iota(jnp.int32, (half, half), 1)
    causal = key <= row
    nothing = jnp.zeros((half, half), jnp.bfloat16)
    score, weight = {}, {}
    for step in range(per_group + 2):
        if step < per_group:
            score[step] = scores_of(keys, q_ref[:, step * HEAD_DIM : (step + 1) * HEAD_DIM])
        head = step - 2
        if head >= 0:
            sums = jnp.dot(values, weight.pop(head), preferred_element_type=jnp.float32)
            out_ref[head] = sums[:HEAD_DIM]
            sum_ref[head : head + 1, :] = sums[HEAD_DIM : HEAD_DIM + 1]
        head = step - 1
        if 0 <= head < per_group:
            raw = score.pop(head)
            early = jnp.where(causal, raw[:half, :half], masked_score)
            before = raw[:half, half:]
            late = jnp.where(causal, raw[half:, half:], masked_score)
            top_early = jnp.max(early, axis=0, keepdims=True) * FOLD
            top_late = jnp.max(jnp.maximum(before, late), axis=0, keepdims=True) * FOLD
            top_ref[head : head + 1, :half] = top_early
            top_ref[head : head + 1, half:] = top_late
            early = jnp.exp2(early * FOLD - top_early).astype(jnp.bfloat16)
            before = jnp.exp2(before * FOLD - top_late).astype(jnp.bfloat16)
            late = jnp.exp2(late * FOLD - top_late).astype(jnp.bfloat16)
            weight[head] = jnp.concatenate(
                [
                    jnp.concatenate([early, before], axis=1),
                    jnp.concatenate([nothing, late], axis=1),
                ],
                axis=0,
            )


def prompt_kernel(per_group, *refs):
    groups_ref, lives_ref, plens_ref, q_ref, own_ref, top_ref, sum_ref, k_ref, v_ref = refs[:9]
    out_ref = refs[-1]
    size = q_ref.shape[0]
    slot = pl.program_id(0)
    live = plens_ref[groups_ref[slot]]
    rows_live = lives_ref[slot]
    keys = k_ref[...].reshape(-1, HEAD_DIM)
    dead = lax.broadcasted_iota(jnp.int32, keys.shape, 0) >= live
    keys = jnp.where(dead, keys[:1].astype(jnp.float32), keys.astype(jnp.float32)).astype(keys.dtype)
    values = with_ones(v_ref[...].reshape(-1, HEAD_DIM))
    dead = lax.broadcasted_iota(jnp.int32, values.shape, 1) >= live
    values = jnp.where(dead, 0.0, values.astype(jnp.float32)).astype(values.dtype)
    kept = lax.broadcasted_iota(jnp.int32, (1, size), 1) < rows_live
    score, weight, rows = {}, {}, {}
    for step in range(per_group + 2):
        if step < per_group:
            score[step] = scores_of(keys, q_ref[:, step * HEAD_DIM : (step + 1) * HEAD_DIM])
        head = step - 2
        if head >= 0:
            sums = jnp.dot(values, weight.pop(head), preferred_element_type=jnp.float32)
            scale = rows.pop(head)
            total = sums[HEAD_DIM : HEAD_DIM + 1] + scale * sum_ref[head : head + 1, :]
            share = jnp.where(kept, 1.0 / total, 0.0)
            result = sums[:HEAD_DIM] * share + own_ref[head] * (scale * share)
            out_ref[:, head * HEAD_DIM : (head + 1) * HEAD_DIM] = jnp.transpose(result).astype(
                out_ref.dtype
            )
        head = step - 1
        if 0 <= head < per_group:
            raw = score.pop(head)
            parts = []
            for part in range(2):
                cols = slice(part * HEAD_DIM, (part + 1) * HEAD_DIM)
                piece = raw[:, cols]
                own_top = top_ref[head : head + 1, cols]
                top = jnp.maximum(jnp.max(piece, axis=0, keepdims=True) * FOLD, own_top)
                parts.append(
                    (
                        jnp.exp2(piece * FOLD - top).astype(jnp.bfloat16),
                        jnp.exp2(own_top - top),
                    )
                )
            weight[head] = jnp.concatenate([p[0] for p in parts], axis=1)
            rows[head] = jnp.concatenate([p[1] for p in parts], axis=1)


def params(mib=60):
    return pltpu.CompilerParams(vmem_limit_bytes=mib * 1024 * 1024)


def fetch_fast(prompt_kv, groups, devices, after):
    slots = groups.shape[0]
    prompt_len = prompt_kv.shape[0]
    rows = 2 * KV_HEADS * TILE
    smem = pl.BlockSpec(memory_space=pltpu.SMEM)
    vmem = pl.BlockSpec(memory_space=pltpu.VMEM)
    anywhere = pl.BlockSpec(memory_space=pl.ANY)
    packed = pl.pallas_call(
        functools.partial(pack_kernel, KV_HEADS, devices),
        out_shape=jax.ShapeDtypeStruct((devices, rows + 8, HEAD_DIM), jnp.bfloat16),
        grid=(KV_HEADS,),
        in_specs=[smem, pl.BlockSpec((prompt_len, 2, HEAD_DIM), lambda h: (0, 0, h))],
        out_specs=pl.BlockSpec((devices, rows + 8, HEAD_DIM), lambda h: (0, 0, 0)),
        name="pack",
    )(groups, prompt_kv)
    with jax.named_scope("spread"):
        spread = lax.all_to_all(packed, "dp", split_axis=0, concat_axis=0, tiled=True)
    chosen = pl.pallas_call(
        functools.partial(select_kernel, slots, rows),
        out_shape=jax.ShapeDtypeStruct((devices, slots, rows, HEAD_DIM), jnp.bfloat16),
        in_specs=[vmem, anywhere],
        out_specs=anywhere,
        scratch_shapes=[
            pltpu.VMEM((devices, HEAD_DIM), jnp.int32),
            pltpu.SMEM((devices, HEAD_DIM), jnp.int32),
            pltpu.SemaphoreType.DMA,
            pltpu.SemaphoreType.DMA((devices, slots)),
        ],
        compiler_params=params(4),
        name="select",
    )(spread, pltpu.with_memory_space_constraint(after, pltpu.HBM))
    with jax.named_scope("send"):
        return lax.all_to_all(chosen, "dp", split_axis=0, concat_axis=0, tiled=True)


def fetch_plain(prompt_kv, groups, devices):
    slots = groups.shape[0]
    prompt_len, _, width = prompt_kv.shape
    sliver = prompt_len // devices
    wanted = lax.all_gather(groups, "dp", axis=0, tiled=True)
    by_prompt = lax.all_to_all(
        prompt_kv.reshape(devices, sliver, 2, width), "dp", split_axis=0, concat_axis=0, tiled=True
    )
    chosen = jnp.take(by_prompt, wanted, axis=0).reshape(devices, slots, sliver, 2, width)
    fetched = lax.all_to_all(chosen, "dp", split_axis=0, concat_axis=0, tiled=True)
    whole = jnp.transpose(fetched, (1, 0, 2, 3, 4))
    whole = whole.reshape(slots, -1, TILE, 2, KV_HEADS, HEAD_DIM)
    whole = jnp.transpose(whole, (1, 0, 3, 4, 2, 5))
    return whole.reshape(whole.shape[0], slots, 2 * KV_HEADS * TILE, HEAD_DIM)


def on_device(queries, resp_kv, prompt_kv, groups, resp_lengths, prompt_lengths):
    devices = lax.axis_size("dp")
    slots = groups.shape[0]
    resp_len = queries.shape[0] // slots
    width = queries.shape[1] // KV_HEADS
    per_group = width // HEAD_DIM
    prompt_len = prompt_kv.shape[0]
    heads = KV_HEADS * per_group
    scores = heads * resp_len * resp_len
    moved = queries.size

    own_shapes = (
        jax.ShapeDtypeStruct((slots, heads, HEAD_DIM, resp_len), jnp.float32),
        jax.ShapeDtypeStruct((slots, heads, resp_len), jnp.float32),
        jax.ShapeDtypeStruct((slots, heads, resp_len), jnp.float32),
    )
    own_steps = []
    for slot in range(slots):
        before = own_steps[-1] if own_steps else ()
        own_steps.append(
            pl.pallas_call(
                functools.partial(own_kernel, per_group),
                grid=(KV_HEADS,),
                out_shape=own_shapes,
                in_specs=[
                    pl.BlockSpec((resp_len, width), lambda c, slot=slot: (slot, c)),
                    pl.BlockSpec((resp_len, 2, HEAD_DIM), lambda c, slot=slot: (slot, 0, c)),
                ]
                + [pl.BlockSpec(memory_space=pl.ANY)] * len(before),
                out_specs=(
                    pl.BlockSpec(
                        (None, per_group, HEAD_DIM, resp_len),
                        lambda c, slot=slot: (slot, c, 0, 0),
                    ),
                    pl.BlockSpec((None, per_group, resp_len), lambda c, slot=slot: (slot, c, 0)),
                    pl.BlockSpec((None, per_group, resp_len), lambda c, slot=slot: (slot, c, 0)),
                ),
                input_output_aliases={2 + i: i for i in range(len(before))},
                compiler_params=params(),
                cost_estimate=pl.CostEstimate(
                    flops=scores * HEAD_DIM * 4,
                    bytes_accessed=moved * 6 // slots,
                    transcendentals=scores,
                ),
                name=f"own{slot}",
            )(queries, resp_kv, *before)
        )
    own = [pltpu.with_memory_space_constraint(part, pltpu.HBM) for part in own_steps[-1]]
    queries = pltpu.with_memory_space_constraint(queries, pltpu.HBM)

    if prompt_len == devices * TILE:
        fetched = fetch_fast(prompt_kv, groups, devices, own_steps[0][1])
    else:
        fetched = fetch_plain(prompt_kv, groups, devices)
    blocks = fetched.shape[0]

    q_spec = pl.BlockSpec((resp_len, width), lambda s, c, *_: (s, c))
    own_spec = pl.BlockSpec((None, per_group, HEAD_DIM, resp_len), lambda s, c, *_: (s, c, 0, 0))
    row_spec = pl.BlockSpec((None, per_group, resp_len), lambda s, c, *_: (s, c, 0))

    def tile_spec(offset):
        return pl.BlockSpec(
            (blocks, None, TILE, HEAD_DIM), lambda s, c, *_: (0, s, c + offset, 0)
        )

    return pl.pallas_call(
        functools.partial(prompt_kernel, per_group),
        grid_spec=pltpu.PrefetchScalarGridSpec(
            num_scalar_prefetch=3,
            grid=(slots, KV_HEADS),
            in_specs=[q_spec, own_spec, row_spec, row_spec, tile_spec(0), tile_spec(KV_HEADS)],
            out_specs=q_spec,
        ),
        out_shape=jax.ShapeDtypeStruct(queries.shape, jnp.bfloat16),
        compiler_params=params(32),
        cost_estimate=pl.CostEstimate(
            flops=slots * scores * HEAD_DIM * 4,
            bytes_accessed=moved * 8,
            transcendentals=slots * scores,
        ),
        name="prompt",
    )(groups, resp_lengths, prompt_lengths, queries, *own, fetched, fetched)


def solution(mesh):
    return jax.shard_map(
        on_device,
        mesh=mesh,
        in_specs=(
            P(("groups", "dp"), None),
            P(("groups", "dp"), None, None),
            P(("groups", "dp"), None, None),
            P(("groups", "dp")),
            P(("groups", "dp")),
            P("groups"),
        ),
        out_specs=P(("groups", "dp"), None),
        check_vma=False,
    )
```

time: 88.5 us -> 71.2 us (0.80)
  waiting for transfers between devices: 0.01 us -> 24.6 us
  blocking collectives: 22 us -> 0 us
  Pallas kernels: 51.5 us -> 34.9 us
  local copies, waits for them, and re-layouts: 8.58 us -> 0.01 us
  starting transfers between devices: 4.9 us -> 10.9 us
    all_to_all x1 -> x0, blocking collectives: 22 us -> none  [fetch_fast(): lax.all_to_all(packed, 'dp', split_axis=0, concat_axis=0, tiled=True)]
    all_to_all x1, waiting for transfers between devices: 0.01 us -> 17.3 us  [fetch_fast(): return lax.all_to_all(chosen, 'dp', split_axis=0, concat_axis=0, tiled=True)]
    pallas_call x3 -> x4, Pallas kernels: 48.7 us -> 33 us  [the longest x2 15.1 us: on_device(): pl.pallas_call(functools.partial(own_kernel, per_group), grid=(KV_HEADS,)...]
    unnamed x16 -> x6, local copies, waits for them, and re-layouts: 8.58 us -> 0.01 us
    all_to_all x0 -> x1, waiting for transfers between devices: none -> 7.27 us  [fetch_fast(): lax.all_to_all(packed, 'dp', split_axis=0, concat_axis=0, tiled=True)]
    all_to_all x0 -> x1, starting transfers between devices: none -> 6.55 us  [fetch_fast(): lax.all_to_all(packed, 'dp', split_axis=0, concat_axis=0, tiled=True)]
  transfers between devices with their start and end apart: 1 -> 2, of which waited for: 0 -> 2; matrix products, arithmetic and copies ran while one was open for 0% -> 0% of each run, Pallas kernels for 26% -> 21%
where the time goes in v1:
time: 71.2 us; the launch traced here: 70.4 us
  Pallas kernels  34.9 us (49%)
  waiting for transfers between devices  24.6 us (35%)
  starting transfers between devices  10.9 us (15%)
    all_to_all x1, waiting for transfers between devices, fetch_fast(): return lax.all_to_all(chosen, 'dp', split_axis=0, concat_axis=0, tiled=True)  17.3 us
    pallas_call x2, Pallas kernels, on_device(): pl.pallas_call(functools.partial(own_kernel, per_group), grid=(KV_HEADS,)...  15.1 us
    pallas_call x1, Pallas kernels, on_device(): pl.pallas_call(functools.partial(prompt_kernel, per_group), grid_spec=plt...  14.2 us
    all_to_all x1, waiting for transfers between devices, fetch_fast(): lax.all_to_all(packed, 'dp', split_axis=0, concat_axis=0, tiled=True)  7.27 us
    all_to_all x1, starting transfers between devices, fetch_fast(): lax.all_to_all(packed, 'dp', split_axis=0, concat_axis=0, tiled=True)  6.55 us
    all_to_all x1, starting transfers between devices, fetch_fast(): return lax.all_to_all(chosen, 'dp', split_axis=0, concat_axis=0, tiled=True)  4.35 us
    pallas_call x1, Pallas kernels, fetch_fast(): pl.pallas_call(functools.partial(pack_kernel, KV_HEADS, devices), out_sha...  3.69 us
    pallas_call x1, Pallas kernels, fetch_fast(): pl.pallas_call(functools.partial(select_kernel, slots, rows), out_shape=j...  1.92 us
  transfers between devices with their start and end apart: 2, of which 2 were waited for; matrix products, arithmetic and copies ran while one was open for 0% of the time, Pallas kernels for 21%

profile of v1, /device:TPU:9, one launch (start us, length us, event | category | flops | bytes accessed | tf_op | source)
XLA Modules:
  0.0 70.4 jit_solution(15123222130176416298)
XLA Ops:
  0.0 3.7 %pack.1 = bf16[16,136,128]{2,1,0:T(8,128)(2,1)} custom-call(s32[2]{0:T(128)} %refs_0_.1, bf16[256,2,512]{2,1,0:T(2,128)(2,1)} %kv_ref.5), custom_call_target="tpu_custom_call" | custom-call | tf_op jit(solution)/shard_map/pack/pallas_call | solution.py:184
  3.7 6.5 %all-to-all-start = ((bf16[16,136,128]{2,1,0:T(8,128)(2,1)}), bf16[16,136,128]{2,1,0:T(8,128)(2,1)S(1)}, u32[]{:S(2)}, u32[]{:S(2)}) async-start(bf16[16,136,128]{2,1,0:T(8,128)(2,1)} %pack.1), calls=%async_computation | async-start | bytes 1114112 | tf_op jit(solution)/shard_map/spread/all_to_all | solution.py:193
  10.2 7.5 %own0.1 = (f32[2,32,128,256]{3,2,1,0:T(8,128)}, f32[2,32,256]{2,1,0:T(8,128)}, f32[2,32,256]{2,1,0:T(8,128)}) custom-call(bf16[512,4096]{1,0:T(8,128)(2,1)} %refs_3_.1, bf16[512,2,512]{2,1,0:T(2,128)(2,1)} %kv_ref.4), custom_call_target="tpu_custom_call" | custom-call | flops 1073741824 | bytes 6291456 | tf_op jit(solution)/shard_map/own0/pallas_call | solution.py:248
  17.8 7.3 %all-to-all-done.in_ref = bf16[16,136,128]{2,1,0:T(8,128)(2,1)S(1)} async-done(((bf16[16,136,128]{2,1,0:T(8,128)(2,1)}), bf16[16,136,128]{2,1,0:T(8,128)(2,1)S(1)}, u32[]{:S(2)}, u32[]{:S(2)}) %all-to-all-start) | async-done | bytes 557088 | tf_op jit(solution)/shard_map/spread/all_to_all | solution.py:193
  25.0 0.0 copy-start
  25.0 0.0 copy-start.1
  25.1 0.0 copy-start.2
  25.1 1.9 %select.1 = bf16[16,2,128,128]{3,2,1,0:T(8,128)(2,1)} custom-call(bf16[16,136,128]{2,1,0:T(8,128)(2,1)S(1)} %all-to-all-done.in_ref, f32[2,32,256]{2,1,0:T(8,128)} %get-tuple-element.12.refs_1_.after_ref), custom_call_target="tpu_custom_call" | custom-call | tf_op jit(solution)/shard_map/select/pallas_call | solution.py:194
  27.0 4.3 %all-to-all-start.1 = ((bf16[16,2,128,128]{3,2,1,0:T(8,128)(2,1)}), bf16[16,2,128,128]{3,2,1,0:T(8,128)(2,1)S(1)}, u32[]{:S(2)}, u32[]{:S(2)}) async-start(bf16[16,2,128,128]{3,2,1,0:T(8,128)(2,1)} %select.1), calls=%async_computation.1 | async-start | bytes 2097152 | tf_op jit(solution)/shard_map/send/all_to_all | solution.py:209
  31.3 7.6 %own1.1 = (f32[2,32,128,256]{3,2,1,0:T(8,128)}, f32[2,32,256]{2,1,0:T(8,128)}, f32[2,32,256]{2,1,0:T(8,128)}) custom-call(bf16[512,4096]{1,0:T(8,128)(2,1)} %refs_3_.1, bf16[512,2,512]{2,1,0:T(2,128)(2,1)} %kv_ref.4, f32[2,32,128,256]{3,2,1,0:T(8,128)} %get-tuple-element.11.refs_0_, ...), custom_call_target="tpu_custom_call", output_to_operand_aliasing={{0}: (2, {}), {1}: (3, {}), {2}: (4, {})} | custom-call | flops 1073741824 | bytes 6291456 | tf_op jit(solution)/shard_map/own1/pallas_call | solution.py:248
  38.9 17.3 %all-to-all-done.1.refs_7_.refs_8_ = bf16[16,2,128,128]{3,2,1,0:T(8,128)(2,1)S(1)} async-done(((bf16[16,2,128,128]{3,2,1,0:T(8,128)(2,1)}), bf16[16,2,128,128]{3,2,1,0:T(8,128)(2,1)S(1)}, u32[]{:S(2)}, u32[]{:S(2)}) %all-to-all-start.1) | async-done | bytes 1048608 | tf_op jit(solution)/shard_map/send/all_to_all | solution.py:209
  56.2 0.0 copy-done
  56.2 0.0 copy-done.1
  56.3 0.0 copy-done.2
  56.3 14.2 %prompt.1 = bf16[512,4096]{1,0:T(8,128)(2,1)} custom-call(s32[2]{0:T(128)S(1)} %copy-done, s32[2]{0:T(128)S(1)} %copy-done.1, s32[16]{0:T(128)S(1)} %copy-done.2, bf16[512,4096]{1,0:T(8,128)(2,1)} %refs_3_.1, f32[2,32,128,256]{3,2,1,0:T(8,128)} %get-tuple-element.14.refs_4_, f32[2,32,256]{2,1,0:T(8,128)} %get-tuple-element.15.refs_5_, ...), custom_call_target="tpu_custom_call" | custom-call | flops 2147483648 | bytes 16777216 | tf_op jit(solution)/shard_map/prompt/pallas_call | solution.py:293
Async XLA Ops:
  3.7 21.4 %all-to-all-start = ((bf16[16,136,128]{2,1,0:T(8,128)(2,1)}), bf16[16,136,128]{2,1,0:T(8,128)(2,1)S(1)}, u32[]{:S(2)}, u32[]{:S(2)}) async-start(bf16[16,136,128]{2,1,0:T(8,128)(2,1)} %pack.1), calls=%async_computation | async-start | bytes 1114112 | tf_op jit(solution)/shard_map/spread/all_to_all | solution.py:193
  25.0 31.2 %copy-start = (s32[2]{0:T(128)S(1)}, s32[2]{0:T(128)}, u32[]{:S(2)}) copy-start(s32[2]{0:T(128)} %refs_0_.1) | copy-start | bytes 28
  25.0 31.2 %copy-start.1 = (s32[2]{0:T(128)S(1)}, s32[2]{0:T(128)}, u32[]{:S(2)}) copy-start(s32[2]{0:T(128)} %refs_1_.1) | copy-start | bytes 28
  25.1 31.2 %copy-start.2 = (s32[16]{0:T(128)S(1)}, s32[16]{0:T(128)}, u32[]{:S(2)}) copy-start(s32[16]{0:T(128)} %refs_2_.1) | copy-start | bytes 196
  27.0 29.3 %all-to-all-start.1 = ((bf16[16,2,128,128]{3,2,1,0:T(8,128)(2,1)}), bf16[16,2,128,128]{3,2,1,0:T(8,128)(2,1)S(1)}, u32[]{:S(2)}, u32[]{:S(2)}) async-start(bf16[16,2,128,128]{3,2,1,0:T(8,128)(2,1)} %select.1), calls=%async_computation.1 | async-start | bytes 2097152 | tf_op jit(solution)/shard_map/send/all_to_all | solution.py:209
